TPU v7x, 512 devices: a whole 4x4x16 slice. The times are simulated.
512 devices in a mesh: dp: 32 (over x, z_hi, core), tensor: 16 (over z_lo, y).
Axes of the slice: x: 4, y: 4, z: 16 (z_hi: 4, z_lo: 4; z = z_hi * 4 + z_lo), core: 2. Of those that a mesh axis runs over, the one named last changes fastest.
Arguments:
- activations: bfloat16 [640, 26624], P('dp', 'tensor'), may hold values from -6 to 6
- weight_codes: int32 [26624, 8192], P(('tensor', 'dp')), may hold values from 0 to 15
- scale_index: int32 [26624, 64], P(('tensor', 'dp')), may hold values from 0 to 15, as said below
- scale_table: float32 [16], replicated
- bit_widths: int32 [1, 26624, 64], P(None, ('tensor', 'dp')), may hold values from 2 to 4
Outputs:
- base_output: bfloat16 [640, 8192], P('tensor', 'dp')
- scores: float32 [1, 640], P(None, 'tensor')
Inputs may be any that keep to these rules, and one draw needn't show every extreme that they name: `scale_index`: an entry of scale_table for each row and each group of 128 columns.
All inputs are finite; a program needn't handle non-finite values.
Results may differ from a plain program's by a relative error of at most 0.0058.
Values may be sent and summed in bfloat16 or wider, within the bound.
No kernel may reach another device: no remote copies, remote signals or barrier semaphores. Data moves between devices by JAX's collectives and lax.ppermute only.
A program may use at most 64 MiB of HBM per device.

v0:
```python
import math
import jax
import jax.numpy as jnp
from jax import lax
from jax.sharding import PartitionSpec as P

HB = 128
NCAND = 1
score_divisor = 512.0


def side_by_side(arrays, axis, split_dim, concat_dim, along):
    columns = [a.reshape(*a.shape[:along], -1) for a in arrays]
    both = jnp.concatenate(columns, axis=along)
    whole, at, done = (
        lax.all_to_all(both, axis, split_axis=split_dim, concat_axis=concat_dim, tiled=True),
        0,
        [],
    )
    for a, column in zip(arrays, columns):
        piece = whole[..., at : at + column.shape[along]]
        done.append(piece.reshape(*piece.shape[:along], *a.shape[along:]))
        at += column.shape[along]
    return tuple(done)


def split_up(value, dim, size):
    before, after = (value.shape[:dim], value.shape[dim + 1 :])
    return jnp.moveaxis(value.reshape(*before, size, -1, *after), dim, 0)


def sum_at_owner(value, axis, dim):
    size = lax.axis_size(axis)
    tiles = lax.all_to_all(split_up(value, dim, size), axis, 0, 0, tiled=True)
    return jnp.sum(tiles, axis=0)


def from_everyone(value, axis):
    size = lax.axis_size(axis)
    return lax.all_to_all(
        jnp.broadcast_to(value[None], (size, *value.shape)), axis, 0, 0, tiled=True
    )


def over_copies(value, axis):
    return from_everyone(value, axis).sum(axis=0)


def sylvester(order_size):
    positions = jnp.arange(order_size, dtype=jnp.int32)
    intersection = positions[:, None] & positions[None, :]
    parity = jnp.zeros((order_size, order_size), jnp.int32)
    for shift_bit in range(max(order_size.bit_length() - 1, 0)):
        parity = parity + (intersection >> shift_bit & 1)
    parity = parity % 2
    return (1 - 2 * parity).astype(jnp.float32)


def dequantize(grouped, index_rows, scale_table, bits_rows):
    one_hot = (index_rows[..., None] == jnp.arange(scale_table.shape[0], dtype=jnp.int32)).astype(
        jnp.float32
    )
    scales = jnp.sum(one_hot * scale_table, axis=-1)
    base_w = ((grouped - 8).astype(jnp.float32) * scales[..., None]).astype(jnp.bfloat16)
    step_size = jnp.where(bits_rows == 2, 4, jnp.where(bits_rows == 3, 2, 1)).astype(jnp.int32)[
        ..., None
    ]
    cand_codes = grouped[None] // step_size * step_size + step_size // 2
    cand_w = ((cand_codes - 8).astype(jnp.float32) * scales[None, :, :, None]).astype(jnp.bfloat16)
    row_count = grouped.shape[0]
    col_count = grouped.shape[1] * grouped.shape[2]
    return jnp.concatenate([base_w[None], cand_w], axis=0).reshape(NCAND + 1, row_count, col_count)


def local(activations, weight_codes, scale_index, scale_table, bit_widths):
    tensor_size = lax.axis_size("tensor")
    tok_rows, feat_width = activations.shape
    block_signs = sylvester(HB).astype(jnp.bfloat16)
    blocked = jnp.einsum(
        "rnb,bc->rnc",
        activations.reshape(tok_rows, feat_width // HB, HB),
        block_signs,
        preferred_element_type=jnp.float32,
    ).reshape(tok_rows, feat_width)
    sign_matrix = sylvester(tensor_size)
    shaped = blocked.reshape(tok_rows, tensor_size, feat_width // tensor_size)
    spread = jnp.einsum(
        "js,rsc->rjc",
        sign_matrix,
        lax.all_to_all(shaped, "tensor", split_axis=1, concat_axis=1, tiled=True),
        precision=lax.Precision.HIGHEST,
    )
    mixed_rows = lax.all_to_all(spread, "tensor", split_axis=1, concat_axis=1, tiled=True).reshape(
        tok_rows, feat_width
    )
    rotated = (mixed_rows * (1.0 / math.sqrt(HB * tensor_size))).astype(jnp.bfloat16)
    all_tokens = lax.all_gather(rotated, "dp", axis=0, tiled=True)
    store_rows, model_width = weight_codes.shape
    group_count = scale_index.shape[1]
    group_width = model_width // group_count
    code_wire = weight_codes.reshape(store_rows, group_count, group_width).astype(jnp.bfloat16)
    index_wire = scale_index.astype(jnp.bfloat16)
    bits_wire = jnp.transpose(bit_widths, (1, 2, 0)).astype(jnp.bfloat16)
    code_home, index_home, bits_home = side_by_side(
        (code_wire, index_wire, bits_wire), "dp", 1, 0, 2
    )
    local_grouped = code_home.astype(jnp.int32)
    local_index = index_home.astype(jnp.int32)
    local_bits = jnp.transpose(bits_home.astype(jnp.int32), (2, 0, 1))
    local_weights = dequantize(local_grouped, local_index, scale_table, local_bits)
    token_sums = sum_at_owner(
        jnp.einsum("tf,kfd->tkd", all_tokens, local_weights, preferred_element_type=jnp.float32),
        "tensor",
        0,
    )
    token_sums = jnp.transpose(token_sums, (1, 0, 2))
    base_rows = token_sums[0]
    cand_diffs = token_sums[1:] - base_rows[None]
    block_scores = jnp.sum(cand_diffs * cand_diffs, axis=2) / score_divisor
    scores = over_copies(block_scores, "dp")
    return (base_rows.astype(jnp.bfloat16), scores)


def solution(mesh):
    in_specs = (
        P("dp", "tensor"),
        P(("tensor", "dp"), None),
        P(("tensor", "dp"), None),
        P(),
        P(None, ("tensor", "dp"), None),
    )
    out_specs = (P("tensor", "dp"), P(None, "tensor"))
    return jax.shard_map(local, mesh=mesh, in_specs=in_specs, out_specs=out_specs, check_vma=False)
```

profile of v0, /device:TPU:1, one launch (start us, length us, event | category | flops | bytes accessed | tf_op | source)
XLA Modules:
  0.0 236.9 jit_solution(8731852525822146054)
XLA Ops:
  7.2 1.0 reshape.173
  8.7 17.6 %all_to_all.38 = f32[20,16,104]{2,0,1:T(8,128)S(1)} all-to-all(f32[20,16,104]{2,0,1:T(8,128)S(1)} %copy.92), channel_id=1, replica_groups=mesh['dp'=32,'tensor'=16] {'tensor'}, dimensions={1} | all-to-all | bytes 266240 | tf_op jit(solution)/shard_map/all_to_all | solution.py:90
  26.6 0.7 copy.94
  27.3 4.4 %all-to-all-start.1 = ((f32[20,16,104]{2,0,1:T(8,128)}), f32[20,16,104]{2,0,1:T(8,128)}, u32[]{:S(2)}, u32[]{:S(2)}) async-start(f32[20,16,104]{2,0,1:T(8,128)} %copy.94), calls=%async_computation.1 | async-start | bytes 393216 | tf_op jit(solution)/shard_map/all_to_all | solution.py:93
  33.8 1.0 copy.133
  34.8 3.5 %reshape.185 = bf16[32,2,6760]{2,1,0:T(2,128)(2,1)} reshape(bf16[64,52,130]{2,1,0:T(8,128)(2,1)S(1)} %bitcast.52) | data formatting | bytes 1730560
  38.3 1.8 all-to-all-done.1
  40.1 18.0 %all-to-all-start.2 = ((bf16[32,2,6760]{2,1,0:T(2,128)(2,1)}), bf16[32,2,6760]{2,1,0:T(2,128)(2,1)S(1)}, u32[]{:S(2)}, u32[]{:S(2)}) async-start(bf16[32,2,6760]{2,1,0:T(2,128)(2,1)} %reshape.185), calls=%async_computation.2 | async-start | bytes 1736704 | tf_op jit(solution)/shard_map/all_to_all | solution.py:16
  58.2 1.0 fusion.16
  59.1 0.8 reshape.176
  59.9 44.8 %all-to-all-done.2 = bf16[32,2,6760]{2,1,0:T(2,128)(2,1)S(1)} async-done(((bf16[32,2,6760]{2,1,0:T(2,128)(2,1)}), bf16[32,2,6760]{2,1,0:T(2,128)(2,1)S(1)}, u32[]{:S(2)}, u32[]{:S(2)}) %all-to-all-start.2) | async-done | bytes 865312 | tf_op jit(solution)/shard_map/all_to_all | solution.py:16
  104.8 3.2 %reshape.186 = bf16[64,52,130]{2,1,0:T(8,128)(2,1)S(1)} reshape(bf16[32,2,6760]{2,1,0:T(2,128)(2,1)S(1)} %all-to-all-done.2) | data formatting | bytes 1730560
  108.0 3.1 %copy.130 = bf16[52,32,2,130]{3,2,1,0:T(2,128)(2,1)} copy(bf16[52,32,2,130]{3,0,2,1:T(8,128)(2,1)S(1)} %bitcast.53) | data formatting | bytes 1730560 | tf_op jit(solution)/shard_map/all_to_all | solution.py:16
  111.1 6.1 %copy.101 = bf16[32,52,2,130]{1,0,3,2:T(8,128)(2,1)S(1)} copy(bf16[32,52,2,130]{3,2,0,1:T(2,128)(2,1)} %bitcast.54) | data formatting | bytes 1730560 | tf_op jit(solution)/shard_map/all_to_all | solution.py:16
  117.2 4.2 %all_to_all.30 = bf16[1664,2,130]{0,2,1:T(8,128)(2,1)S(1)} reshape(bf16[32,52,2,130]{1,0,3,2:T(8,128)(2,1)S(1)} %copy.101) | data formatting | bytes 1730560 | tf_op jit(solution)/shard_map/all_to_all | solution.py:16
  121.6 17.6 %fusion.10 = (bf16[1664,2,128]{0,2,1:T(8,128)(2,1)S(1)}, bf16[1664,2,128]{0,2,1:T(8,128)(2,1)S(1)}) fusion(f32[1664,2]{0,1:T(2,128)S(1)} %select_reduce_fusion, bf16[1664,2,130]{0,2,1:T(8,128)(2,1)S(1)} %all_to_all.30, s32[1664,2]{0,1:T(2,128)S(1)} %get-tuple-element.5, s32[1664,2]{0,1:T(2,128)S(1)} %bitcast.62, s32[1664,2]{0,1:T(2,128)S(1)} %get-tuple-element.4), kind=kLoop, calls=%fused_computation.15 | loop fusion | flops 8093696 | bytes 2609152 | tf_op jit(solution)/shard_map/convert_element_type | solution.py:64
  139.8 1.3 copy.108
  141.1 20.7 %all-gather.3.cloned.1.call-done = bf16[32,20,1664]{2,1,0:T(8,128)(2,1)} async-done(((bf16[1,20,1664]{2,1,0:T(8,128)(2,1)}), bf16[32,20,1664]{2,1,0:T(8,128)(2,1)}) %all-gather.3.cloned.1.call-update) | async-done | bytes 2129936 | tf_op jit(solution)/shard_map/all_gather | solution.py:97
  161.8 2.6 %reshape.182 = bf16[16,40,1664,1]{2,1,0,3:T(8,128)(2,1)S(1)} reshape(bf16[32,20,1664]{2,1,0:T(8,128)(2,1)} %all-gather.3.cloned.1.call-done) | data formatting | bytes 4259840 | tf_op jit(solution)/shard_map/tf,kfd->tkd/dot_general | solution.py:112
  164.4 2.5 %fusion = f32[16,40,2,256]{3,1,2,0:T(8,128)S(1)} fusion(bf16[16,40,1664,1]{2,1,0,3:T(8,128)(2,1)S(1)} %reshape.182, bf16[1,1664,256]{2,1,0:T(8,128)(2,1)} %copy.108, bf16[1,1664,256]{2,1,0:T(8,128)(2,1)S(1)} %copy.107), kind=kOutput, calls=%fused_computation.5 | convolution fusion | flops 1093926912 | bytes 5144576 | tf_op jit(solution)/shard_map/tf,kfd->tkd/dot_general | solution.py:112
  167.0 36.0 %all_to_all.39 = f32[16,40,2,256]{3,1,2,0:T(8,128)S(1)} all-to-all(f32[16,40,2,256]{3,1,2,0:T(8,128)S(1)} %fusion), channel_id=1, replica_groups=mesh['dp'=32,'tensor'=16] {'tensor'}, dimensions={0} | all-to-all | bytes 2621440 | tf_op jit(solution)/shard_map/all_to_all | solution.py:34
  203.2 0.6 broadcast_in_dim.17
  203.8 11.5 %all-to-all-start.4 = ((f32[32,1,40]{2,1,0:T(1,128)}), f32[32,1,40]{2,1,0:T(1,128)S(1)}, u32[]{:S(2)}, u32[]{:S(2)}) async-start(f32[32,1,40]{2,1,0:T(1,128)} %broadcast_in_dim.17), calls=%async_computation.4 | async-start | bytes 32768 | tf_op jit(solution)/shard_map/all_to_all | solution.py:40
  216.0 13.6 %all-to-all-done.4 = f32[32,1,40]{2,1,0:T(1,128)S(1)} async-done(((f32[32,1,40]{2,1,0:T(1,128)}), f32[32,1,40]{2,1,0:T(1,128)S(1)}, u32[]{:S(2)}, u32[]{:S(2)}) %all-to-all-start.4) | async-done | bytes 5152 | tf_op jit(solution)/shard_map/all_to_all | solution.py:40
  (35 shorter events, 5.0 us)
Async XLA Ops:
  7.2 24.6 %copy-start.2 = (s32[1,52,64]{2,0,1:T(1,128)S(1)}, s32[1,52,64]{2,0,1:T(1,128)}, u32[]{:S(2)}) copy-start(s32[1,52,64]{2,0,1:T(1,128)} %param.9) | copy-start | bytes 39940
  8.4 23.9 %copy-start.1 = (s32[52,64]{1,0:T(8,128)S(1)}, s32[52,64]{1,0:T(8,128)}, u32[]{:S(2)}) copy-start(s32[52,64]{1,0:T(8,128)} %param.7) | copy-start | bytes 39940
  8.7 24.1 %copy-start = (s32[52,8192]{1,0:T(8,128)S(1)}, s32[52,8192]{1,0:T(8,128)}, u32[]{:S(2)}) copy-start(s32[52,8192]{1,0:T(8,128)} %param.6) | copy-start | bytes 5111812
  27.3 12.8 %all-to-all-start.1 = ((f32[20,16,104]{2,0,1:T(8,128)}), f32[20,16,104]{2,0,1:T(8,128)}, u32[]{:S(2)}, u32[]{:S(2)}) async-start(f32[20,16,104]{2,0,1:T(8,128)} %copy.94), calls=%async_computation.1 | async-start | bytes 393216 | tf_op jit(solution)/shard_map/all_to_all | solution.py:93
  40.1 64.7 %all-to-all-start.2 = ((bf16[32,2,6760]{2,1,0:T(2,128)(2,1)}), bf16[32,2,6760]{2,1,0:T(2,128)(2,1)S(1)}, u32[]{:S(2)}, u32[]{:S(2)}) async-start(bf16[32,2,6760]{2,1,0:T(2,128)(2,1)} %reshape.185), calls=%async_computation.2 | async-start | bytes 1736704 | tf_op jit(solution)/shard_map/all_to_all | solution.py:16
  58.1 103.7 %all-gather.3.cloned.1.call-start = ((), (), s32[]{:S(2)}) async-start(), calls=%async_computation.5 | async-start | bytes 2635776 | tf_op jit(solution)/shard_map/all_gather | solution.py:97
  117.2 4.3 %copy-start.3 = (f32[16]{0:T(128)S(1)}, f32[16]{0:T(128)}, u32[]{:S(2)}) copy-start(f32[16]{0:T(128)} %param.8) | copy-start | bytes 196
  203.8 25.7 %all-to-all-start.4 = ((f32[32,1,40]{2,1,0:T(1,128)}), f32[32,1,40]{2,1,0:T(1,128)S(1)}, u32[]{:S(2)}, u32[]{:S(2)}) async-start(f32[32,1,40]{2,1,0:T(1,128)} %broadcast_in_dim.17), calls=%async_computation.4 | async-start | bytes 32768 | tf_op jit(solution)/shard_map/all_to_all | solution.py:40
Sparse Core Ops, SparseCore 0:
  62.0 99.7 all-gather.2
where the time goes:
time: 238 us; the launch traced here: 237 us
  waiting for transfers between devices  81 us (34%)
  blocking collectives  53.6 us (23%)
  starting transfers between devices  33.9 us (14%)
  local copies, waits for them, and re-layouts  30.9 us (13%)
  other arithmetic  20.1 us (8%)
  between operations  14.3 us (6%)
  matrix products  3.08 us (1%)
    all_to_all x1, waiting for transfers between devices, side_by_side(): lax.all_to_all(both, axis, split_axis=split_dim, concat_axis=concat_dim,...  44.8 us
    all_to_all x1, blocking collectives, sum_at_owner(): tiles = lax.all_to_all(split_up(value, dim, size), axis, 0, 0, tiled=True)  36 us
    all_gather x1, waiting for transfers between devices, local(): all_tokens = lax.all_gather(rotated, 'dp', axis=0, tiled=True)  20.7 us
    all_to_all x1, starting transfers between devices, side_by_side(): lax.all_to_all(both, axis, split_axis=split_dim, concat_axis=concat_dim,...  18 us
    all_to_all x1, blocking collectives, local(): lax.all_to_all(shaped, 'tensor', split_axis=1, concat_axis=1, tiled=True)  17.6 us
    convert_element_type x1, other arithmetic, dequantize(): ((grouped - 8).astype(jnp.float32) * scales[..., None]).astype(jnp.bfloat16)  17.6 us
    all_to_all x1, waiting for transfers between devices, from_everyone(): lax.all_to_all(jnp.broadcast_to(value[None], (size, *value.shape)), axis,...  13.6 us
    all_to_all x3, local copies, waits for them, and re-layouts, side_by_side(): lax.all_to_all(both, axis, split_axis=split_dim, concat_axis=concat_dim,...  13.3 us
  transfers between devices with their start and end apart: 4, of which 4 were waited for; matrix products, arithmetic and copies ran while one was open for 17% of the time, Pallas kernels for 0%

commit v1 on v0

--- a/solution.py
+++ b/solution.py
@@ -3,6 +3,7 @@
 import jax.numpy as jnp
 from jax import lax
 from jax.sharding import PartitionSpec as P
+from jax.lax import all_to_all, axis_size
 
 HB = 128
 NCAND = 1
@@ -94,7 +95,15 @@
         tok_rows, feat_width
     )
     rotated = (mixed_rows * (1.0 / math.sqrt(HB * tensor_size))).astype(jnp.bfloat16)
-    all_tokens = lax.all_gather(rotated, "dp", axis=0, tiled=True)
+    all_tokens = jnp.concatenate(
+        all_to_all(
+            jnp.stack([rotated for _ in range(axis_size("dp"))], axis=0),
+            concat_axis=0,
+            axis_name="dp",
+            split_axis=0,
+        ),
+        axis=0,
+    )
     store_rows, model_width = weight_codes.shape
     group_count = scale_index.shape[1]
     group_width = model_width // group_count

time: 238 us -> 292 us (1.23)
  waiting for transfers between devices: 81 us -> 129 us
  between operations: 14.3 us -> 0.88 us
  starting transfers between devices: 33.9 us -> 41.3 us
  local copies, waits for them, and re-layouts: 30.9 us -> 37.3 us
  blocking collectives: 53.6 us -> 57.4 us
    all_to_all x0 -> x1, waiting for transfers between devices: none -> 71.6 us  [local(): all_to_all(jnp.stack([rotated for _ in range(axis_size('dp'))], axis=0),...]
    all_gather x1 -> x0, waiting for transfers between devices: 20.7 us -> none  [local(): all_tokens = lax.all_gather(rotated, 'dp', axis=0, tiled=True)]
    all_to_all x0 -> x1, starting transfers between devices: none -> 9.86 us  [local(): all_to_all(jnp.stack([rotated for _ in range(axis_size('dp'))], axis=0),...]
    all_to_all x1, blocking collectives: 36 us -> 39.9 us  [sum_at_owner(): tiles = lax.all_to_all(split_up(value, dim, size), axis, 0, 0, tiled=True)]
    all_to_all x3, local copies, waits for them, and re-layouts: 13.3 us -> 16.6 us  [side_by_side(): lax.all_to_all(both, axis, split_axis=split_dim, concat_axis=concat_dim,...]
    unnamed x14 -> x17, local copies, waits for them, and re-layouts: 7.79 us -> 8 us
  transfers between devices with their start and end apart: 4 -> 4, of which waited for: 4 -> 4; matrix products, arithmetic and copies ran while one was open for 17% -> 16% of each run, Pallas kernels for 0% -> 0%
where the time goes in v1:
time: 292 us; the launch traced here: 291 us
  waiting for transfers between devices  129 us (44%)
  blocking collectives  57.4 us (20%)
  starting transfers between devices  41.3 us (14%)
  local copies, waits for them, and re-layouts  37.3 us (13%)
  other arithmetic  21 us (7%)
  matrix products  3.71 us (1%)
    all_to_all x1, waiting for transfers between devices, local(): all_to_all(jnp.stack([rotated for _ in range(axis_size('dp'))], axis=0),...  71.6 us
    all_to_all x1, waiting for transfers between devices, side_by_side(): lax.all_to_all(both, axis, split_axis=split_dim, concat_axis=concat_dim,...  42.2 us
    all_to_all x1, blocking collectives, sum_at_owner(): tiles = lax.all_to_all(split_up(value, dim, size), axis, 0, 0, tiled=True)  39.9 us
    convert_element_type x1, other arithmetic, dequantize(): ((grouped - 8).astype(jnp.float32) * scales[..., None]).astype(jnp.bfloat16)  18.4 us
    all_to_all x1, starting transfers between devices, side_by_side(): lax.all_to_all(both, axis, split_axis=split_dim, concat_axis=concat_dim,...  18 us
    all_to_all x1, blocking collectives, local(): lax.all_to_all(shaped, 'tensor', split_axis=1, concat_axis=1, tiled=True)  17.6 us
    all_to_all x3, local copies, waits for them, and re-layouts, side_by_side(): lax.all_to_all(both, axis, split_axis=split_dim, concat_axis=concat_dim,...  16.6 us
    all_to_all x1, waiting for transfers between devices, from_everyone(): lax.all_to_all(jnp.broadcast_to(value[None], (size, *value.shape)), axis,...  13.6 us
  transfers between devices with their start and end apart: 4, of which 4 were waited for; matrix products, arithmetic and copies ran while one was open for 16% of the time, Pallas kernels for 0%

profile of v1, /device:TPU:1, one launch (start us, length us, event | category | flops | bytes accessed | tf_op | source)
XLA Modules:
  0.0 290.8 jit_solution(16260657567598703817)
XLA Ops:
  0.6 1.0 reshape.178
  2.2 17.6 %all_to_all.43 = f32[20,16,104]{2,0,1:T(8,128)S(1)} all-to-all(f32[20,16,104]{2,0,1:T(8,128)S(1)} %copy.92), channel_id=1, replica_groups=mesh['dp'=32,'tensor'=16] {'tensor'}, dimensions={1} | all-to-all | bytes 266240 | tf_op jit(solution)/shard_map/all_to_all | solution.py:91
  20.8 4.4 %all-to-all-start.1 = ((f32[20,16,104]{2,0,1:T(8,128)}), f32[20,16,104]{2,0,1:T(8,128)}, u32[]{:S(2)}, u32[]{:S(2)}) async-start(f32[20,16,104]{2,0,1:T(8,128)} %copy.94), calls=%async_computation.1 | async-start | bytes 393216 | tf_op jit(solution)/shard_map/all_to_all | solution.py:94
  27.3 1.0 copy.133
  28.2 3.5 %reshape.186 = bf16[32,2,6760]{2,1,0:T(2,128)(2,1)} reshape(bf16[64,52,130]{2,1,0:T(8,128)(2,1)S(1)} %bitcast.52) | data formatting | bytes 1730560
  31.8 1.8 all-to-all-done.1
  33.6 18.0 %all-to-all-start.3 = ((bf16[32,2,6760]{2,1,0:T(2,128)(2,1)}), bf16[32,2,6760]{2,1,0:T(2,128)(2,1)S(1)}, u32[]{:S(2)}, u32[]{:S(2)}) async-start(bf16[32,2,6760]{2,1,0:T(2,128)(2,1)} %reshape.186), calls=%async_computation.3 | async-start | bytes 1736704 | tf_op jit(solution)/shard_map/all_to_all | solution.py:17
  51.6 1.0 fusion.16
  52.7 42.2 %all-to-all-done.3 = bf16[32,2,6760]{2,1,0:T(2,128)(2,1)S(1)} async-done(((bf16[32,2,6760]{2,1,0:T(2,128)(2,1)}), bf16[32,2,6760]{2,1,0:T(2,128)(2,1)S(1)}, u32[]{:S(2)}, u32[]{:S(2)}) %all-to-all-start.3) | async-done | bytes 865312 | tf_op jit(solution)/shard_map/all_to_all | solution.py:17
  94.9 1.7 stack.2
  96.5 9.9 %all-to-all-start.2 = ((bf16[32,20,1664]{2,1,0:T(8,128)(2,1)}), bf16[32,20,1664]{2,1,0:T(8,128)(2,1)S(1)}, u32[]{:S(2)}, u32[]{:S(2)}) async-start(bf16[32,20,1664]{2,1,0:T(8,128)(2,1)} %stack.2), calls=%async_computation.2 | async-start | bytes 5111808 | tf_op jit(solution)/shard_map/all_to_all | solution.py:99
  106.4 4.2 %reshape.187 = bf16[64,52,130]{2,1,0:T(8,128)(2,1)} reshape(bf16[32,2,6760]{2,1,0:T(2,128)(2,1)S(1)} %all-to-all-done.3) | data formatting | bytes 1730560
  110.6 4.6 %copy.130 = bf16[52,32,2,130]{3,2,1,0:T(2,128)(2,1)} copy(bf16[52,32,2,130]{3,0,2,1:T(8,128)(2,1)} %bitcast.53) | data formatting | bytes 1730560 | tf_op jit(solution)/shard_map/all_to_all | solution.py:17
  115.2 6.9 %copy.101 = bf16[32,52,2,130]{1,0,3,2:T(8,128)(2,1)} copy(bf16[32,52,2,130]{3,2,0,1:T(2,128)(2,1)} %bitcast.54) | data formatting | bytes 1730560 | tf_op jit(solution)/shard_map/all_to_all | solution.py:17
  122.1 5.1 %all_to_all.34 = bf16[1664,2,130]{0,2,1:T(8,128)(2,1)S(1)} reshape(bf16[32,52,2,130]{1,0,3,2:T(8,128)(2,1)} %copy.101) | data formatting | bytes 1730560 | tf_op jit(solution)/shard_map/all_to_all | solution.py:17
  127.5 18.4 %fusion.10 = (bf16[1664,2,128]{0,2,1:T(8,128)(2,1)}, bf16[1664,2,128]{0,2,1:T(8,128)(2,1)}) fusion(f32[1664,2]{0,1:T(2,128)S(1)} %select_reduce_fusion, bf16[1664,2,130]{0,2,1:T(8,128)(2,1)S(1)} %all_to_all.34, s32[1664,2]{0,1:T(2,128)S(1)} %get-tuple-element.5, s32[1664,2]{0,1:T(2,128)S(1)} %bitcast.62, s32[1664,2]{0,1:T(2,128)S(1)} %get-tuple-element.4), kind=kLoop, calls=%fused_computation.15 | loop fusion | flops 8093696 | bytes 2609152 | tf_op jit(solution)/shard_map/convert_element_type | solution.py:65
  145.9 2.3 copy.108
  148.2 1.3 copy.107
  149.5 71.6 %all-to-all-done.2 = bf16[32,20,1664]{2,1,0:T(8,128)(2,1)S(1)} async-done(((bf16[32,20,1664]{2,1,0:T(8,128)(2,1)}), bf16[32,20,1664]{2,1,0:T(8,128)(2,1)S(1)}, u32[]{:S(2)}, u32[]{:S(2)}) %all-to-all-start.2) | async-done | bytes 2129952 | tf_op jit(solution)/shard_map/all_to_all | solution.py:99
  221.1 2.1 reshape.183
  223.1 3.2 %fusion = f32[16,40,2,256]{3,1,2,0:T(8,128)S(1)} fusion(bf16[16,40,1664,1]{2,1,0,3:T(8,128)(2,1)} %reshape.183, bf16[1,1664,256]{2,1,0:T(8,128)(2,1)S(1)} %copy-done.2, bf16[1,1664,256]{2,1,0:T(8,128)(2,1)} %copy.107), kind=kOutput, calls=%fused_computation.5 | convolution fusion | flops 1093926912 | bytes 5144576 | tf_op jit(solution)/shard_map/tf,kfd->tkd/dot_general | solution.py:121
  226.3 39.9 %all_to_all.44 = f32[16,40,2,256]{3,1,2,0:T(8,128)S(1)} all-to-all(f32[16,40,2,256]{3,1,2,0:T(8,128)S(1)} %fusion), channel_id=1, replica_groups=mesh['dp'=32,'tensor'=16] {'tensor'}, dimensions={0} | all-to-all | bytes 2621440 | tf_op jit(solution)/shard_map/all_to_all | solution.py:35
  267.0 9.1 %all-to-all-start.5 = ((f32[32,1,40]{2,1,0:T(1,128)}), f32[32,1,40]{2,1,0:T(1,128)S(1)}, u32[]{:S(2)}, u32[]{:S(2)}) async-start(f32[32,1,40]{2,1,0:T(1,128)} %broadcast_in_dim.17), calls=%async_computation.5 | async-start | bytes 32768 | tf_op jit(solution)/shard_map/all_to_all | solution.py:41
  276.6 13.6 %all-to-all-done.5 = f32[32,1,40]{2,1,0:T(1,128)S(1)} async-done(((f32[32,1,40]{2,1,0:T(1,128)}), f32[32,1,40]{2,1,0:T(1,128)S(1)}, u32[]{:S(2)}, u32[]{:S(2)}) %all-to-all-start.5) | async-done | bytes 5152 | tf_op jit(solution)/shard_map/all_to_all | solution.py:41
  (39 shorter events, 5.9 us)
Async XLA Ops:
  0.6 24.6 %copy-start.4 = (s32[1,52,64]{2,0,1:T(1,128)S(1)}, s32[1,52,64]{2,0,1:T(1,128)}, u32[]{:S(2)}) copy-start(s32[1,52,64]{2,0,1:T(1,128)} %param.9) | copy-start | bytes 39940
  1.9 23.9 %copy-start.3 = (s32[52,64]{1,0:T(8,128)S(1)}, s32[52,64]{1,0:T(8,128)}, u32[]{:S(2)}) copy-start(s32[52,64]{1,0:T(8,128)} %param.7) | copy-start | bytes 39940
  2.2 24.1 %copy-start.1 = (s32[52,8192]{1,0:T(8,128)S(1)}, s32[52,8192]{1,0:T(8,128)}, u32[]{:S(2)}) copy-start(s32[52,8192]{1,0:T(8,128)} %param.6) | copy-start | bytes 5111812
  20.8 12.8 %all-to-all-start.1 = ((f32[20,16,104]{2,0,1:T(8,128)}), f32[20,16,104]{2,0,1:T(8,128)}, u32[]{:S(2)}, u32[]{:S(2)}) async-start(f32[20,16,104]{2,0,1:T(8,128)} %copy.94), calls=%async_computation.1 | async-start | bytes 393216 | tf_op jit(solution)/shard_map/all_to_all | solution.py:94
  33.6 61.3 %all-to-all-start.3 = ((bf16[32,2,6760]{2,1,0:T(2,128)(2,1)}), bf16[32,2,6760]{2,1,0:T(2,128)(2,1)S(1)}, u32[]{:S(2)}, u32[]{:S(2)}) async-start(bf16[32,2,6760]{2,1,0:T(2,128)(2,1)} %reshape.186), calls=%async_computation.3 | async-start | bytes 1736704 | tf_op jit(solution)/shard_map/all_to_all | solution.py:17
  96.5 124.5 %all-to-all-start.2 = ((bf16[32,20,1664]{2,1,0:T(8,128)(2,1)}), bf16[32,20,1664]{2,1,0:T(8,128)(2,1)S(1)}, u32[]{:S(2)}, u32[]{:S(2)}) async-start(bf16[32,20,1664]{2,1,0:T(8,128)(2,1)} %stack.2), calls=%async_computation.2 | async-start | bytes 5111808 | tf_op jit(solution)/shard_map/all_to_all | solution.py:99
  122.1 5.2 %copy-start.5 = (f32[16]{0:T(128)S(1)}, f32[16]{0:T(128)}, u32[]{:S(2)}) copy-start(f32[16]{0:T(128)} %param.8) | copy-start | bytes 196
  145.9 2.3 copy-start
  149.5 73.6 %copy-start.2 = (bf16[1,1664,256]{2,1,0:T(8,128)(2,1)S(1)}, bf16[1,1664,256]{2,1,0:T(8,128)(2,1)}, u32[]{:S(2)}) copy-start(bf16[1,1664,256]{2,1,0:T(8,128)(2,1)} %copy.108) | copy-start | bytes 2555908
  267.0 23.3 %all-to-all-start.5 = ((f32[32,1,40]{2,1,0:T(1,128)}), f32[32,1,40]{2,1,0:T(1,128)S(1)}, u32[]{:S(2)}, u32[]{:S(2)}) async-start(f32[32,1,40]{2,1,0:T(1,128)} %broadcast_in_dim.17), calls=%async_computation.5 | async-start | bytes 32768 | tf_op jit(solution)/shard_map/all_to_all | solution.py:41
